TPU v7x, 256 devices: a whole 4x4x8 slice. The times are simulated.
256 devices in a mesh: box: 64 (over x, z, core), col: 4 (over y).
Axes of the slice: x: 4, y: 4, z: 8, core: 2. Of those that a mesh axis runs over, the one named last changes fastest.
Arguments:
- leaf_maps: float32 [64, 1024, 1024], P('box', None, 'col'), as said below
- leaf_nodes: int32 [64, 4, 256], P('box'), may hold values from 0 to 255, each once within a row
Outputs:
- top_maps: float32 [64, 1024, 1024], P('box', None, 'col')
Inputs may be any that keep to these rules, and one draw needn't show every extreme that they name: `leaf_maps`: each leaf map is symmetric and positive definite. `leaf_nodes`: for each leaf and side, the entries are a permutation of 0 to 255.
All inputs are finite; a program needn't handle non-finite values.
Results may differ from a plain program's by a relative error of at most 0.0003.
Values sent between devices are 32-bit elements; how exact they have to be, the bound alone decides.
No kernel may reach another device: no remote copies, remote signals or barrier semaphores. Data moves between devices by JAX's collectives and lax.ppermute only.
A program may use at most 64 MiB of HBM per device.

v0:
```python
import jax
import jax.numpy as jnp
from jax import lax
from jax.experimental import pallas as pl
from jax.experimental.pallas import tpu as pltpu
from jax.sharding import PartitionSpec as P


Q = 256
F32 = jnp.float32
BF16 = jnp.bfloat16
HIGHEST = lax.Precision.HIGHEST
VMEM = pl.BlockSpec(memory_space=pltpu.VMEM)
SMEM = pl.BlockSpec(memory_space=pltpu.SMEM)
ANY = pl.BlockSpec(memory_space=pl.ANY)


def dot(a, b):
    return jnp.dot(a, b, precision=HIGHEST, preferred_element_type=F32)


def dot_t(a, b):
    return lax.dot_general(
        a, b, (((1,), (1,)), ((), ())), precision=HIGHEST, preferred_element_type=F32
    )


def split(x):
    high = x.astype(BF16)
    return high, (x - high.astype(F32)).astype(BF16)


def dot3(a, b, b_dim=0):
    (a1, a2), (b1, b2) = split(a), split(b)

    def mul(p, q):
        return lax.dot_general(p, q, (((1,), (b_dim,)), ((), ())), preferred_element_type=F32)

    return mul(a1, b1) + (mul(a1, b2) + mul(a2, b1))


def row_of(x, j):
    return jnp.broadcast_to(x[j : j + 1, :], (8, 128))


def col_of(x, j):
    return jnp.broadcast_to(x[:, j : j + 1], (8, 128))


def eliminate(rows, tile, base, lane, sub):
    cols = [col_of(rows[tile], base + j) for j in range(8)]
    rows = list(rows)
    for j in range(0, 8, 2):
        c0, c1 = cols[j], cols[j + 1]
        a, b2 = row_of(c0, j), row_of(c1, j)
        b, c = row_of(c0, j + 1), row_of(c1, j + 1)
        rd = 1.0 / (a * c - b * b2)
        l0, l1 = lane == base + j, lane == base + j + 1
        s0, s1 = sub == j, sub == j + 1

        def scaled(x):
            r0, r1 = row_of(x, j), row_of(x, j + 1)
            return (c * r0 - b2 * r1) * rd, (a * r1 - b * r0) * rd

        def put(old, n0, n1):
            return jnp.where(s0, n0, jnp.where(s1, n1, old - (c0 * n0 + c1 * n1)))

        for m in range(j + 2, 8):
            cols[m] = put(cols[m], *scaled(cols[m]))
        for i in range(len(rows)):
            n0, n1 = scaled(rows[i])
            old = rows[i]
            if i == tile:
                n0 = jnp.where(l0, c * rd, jnp.where(l1, -(b2 * rd), n0))
                n1 = jnp.where(l0, -(b * rd), jnp.where(l1, a * rd, n1))
                old = jnp.where(l0 | l1, 0.0, old)
            rows[i] = put(old, n0, n1)
    return rows


def update(rows, pivots, tile, base, in_block):
    cols = [col_of(rows[tile], base + j) for j in range(8)]
    out = []
    for i in range(len(rows)):
        x = jnp.where(in_block, 0.0, rows[i]) if i == tile else rows[i]
        p = [cols[j] * pivots[i][j] for j in range(8)]
        out.append(x - (((p[0] + p[1]) + (p[2] + p[3])) + ((p[4] + p[5]) + (p[6] + p[7]))))
    return out


def invert(A, w=32):
    n = A.shape[0]
    x = A[...]
    on_diagonal = lax.broadcasted_iota(jnp.int32, (n, n), 0) == lax.broadcasted_iota(jnp.int32, (n, n), 1)
    across = lax.rsqrt(jnp.sum(jnp.where(on_diagonal, x, 0.0), axis=0, keepdims=True))
    down = jnp.broadcast_to(across, (8, n)).T[:, 0:1]
    A[...] = x * down * across
    eliminate_all(A, w)
    A[...] = A[...] * down * across


def eliminate_all(A, w):
    n = A.shape[0]
    tiles, groups_in = n // 128, w // 8
    lane = lax.broadcasted_iota(jnp.int32, (8, 128), 1)
    sub = lax.broadcasted_iota(jnp.int32, (8, 128), 0)
    wide = lax.broadcasted_iota(jnp.int32, (1, n), 1)
    panel = A[0:w, :]
    for r0 in range(0, n, w):
        tile, b0 = r0 // 128, r0 % 128
        groups = [
            [panel[g * 8 : g * 8 + 8, i * 128 : i * 128 + 128] for i in range(tiles)]
            for g in range(groups_in)
        ]
        for b in range(groups_in):
            base = b0 + b * 8
            in_block = (lane >= base) & (lane < base + 8)
            done = eliminate(groups[b], tile, base, lane, sub)
            pivots = [[row_of(done[i], j) for j in range(8)] for i in range(tiles)]
            groups[b] = done
            for g in list(range(b + 1, groups_in)) + list(range(b)):
                groups[g] = update(groups[g], pivots, tile, base, in_block)
        final = jnp.concatenate([jnp.concatenate(g, axis=1) for g in groups], axis=0)
        in_panel = (wide >= r0) & (wide < r0 + w)

        def trail(lo, hi):
            x = A[lo:hi, :]
            return jnp.where(in_panel, 0.0, x) - dot(x[:, r0 : r0 + w], final)

        nxt = r0 + w
        if nxt < n:
            panel = trail(nxt, nxt + w)
            if nxt + w < n:
                A[nxt + w : n, :] = trail(nxt + w, n)
        if r0 > 0:
            A[0:r0, :] = trail(0, r0)
        A[r0:nxt, :] = final


def call(kernel, out_shape, in_specs, flops, scratch=(), limit=None):
    outs = [jax.ShapeDtypeStruct(s, F32) for s in out_shape]
    return pl.pallas_call(
        kernel,
        out_shape=outs,
        in_specs=in_specs,
        out_specs=[VMEM] * len(outs),
        scratch_shapes=list(scratch),
        cost_estimate=pl.CostEstimate(flops=flops, bytes_accessed=1 << 20, transcendentals=0),
        compiler_params=pltpu.CompilerParams(vmem_limit_bytes=limit or (40 << 20)),
    )


def one_hot(table, k):
    lanes = lax.broadcasted_iota(jnp.int32, (Q, Q), 1)
    return jnp.where(lanes == jnp.broadcast_to(table[:, k : k + 1], (Q, Q)), 1.0, 0.0).astype(BF16)


def picked(nodes, sides):
    picks = [nodes[pl.ds(s, 1), :] for s in sides]
    return jnp.concatenate(picks + [jnp.zeros((8 - len(sides), Q), jnp.int32)], axis=0).T


def mul(a, b):
    return jnp.dot(a, b, preferred_element_type=F32)


def mul_t(a, b):
    return lax.dot_general(a, b, (((1,), (1,)), ((), ())), preferred_element_type=F32)


def pieces(x):
    x1 = x.astype(BF16)
    rest = x - x1.astype(F32)
    x2 = rest.astype(BF16)
    return x1, x2, (rest - x2.astype(F32)).astype(BF16)


def permute_kernel(role, panel, nodes, u_out, d_out):
    sides = [role[1], role[2], role[3], role[4]]
    table = picked(nodes, sides + [role[0]])
    to_own = one_hot(table, 4)
    for k in range(4):
        hot = one_hot(table, k)
        x = panel[pl.ds(pl.multiple_of(sides[k] * Q, Q), Q), :]
        parts = [mul(hot, piece).astype(BF16) for piece in pieces(x)]
        if k < 2:
            moved = [mul_t(to_own, piece) for piece in parts]
        else:
            moved = [mul_t(piece, to_own) for piece in parts]
        to = u_out if k < 2 else d_out
        to[:, k % 2 * Q : k % 2 * Q + Q] = moved[0] + (moved[1] + moved[2])


def reorder(x, rows, cols):
    parts = [mul_t(mul(rows, piece).astype(BF16), cols) for piece in pieces(x)]
    return parts[0] + (parts[1] + parts[2])


def coupling_kernel(role, raw, g1, g2, g3, nodes, out):
    hot = one_hot(picked(nodes, [role[1]]), 0)
    out[...] = reorder(jnp.where(role[0] == role[1], raw[...], g1[...] + (g2[...] + g3[...])), hot, hot)


def inner_kernel(role, raw, g1, g2, g3, nodes, out):
    table = picked(nodes, [role[1], role[2]])
    hot_a, hot_c = one_hot(table, 0), one_hot(table, 1)

    def block(side):
        shift = (role[0] - side + 4) % 4
        a = jnp.where(shift == 0, raw[...], g1[...])
        b = jnp.where(shift == 2, g2[...], g3[...])
        return jnp.where(shift < 2, a, b)

    out[:, :Q] = reorder(block(role[1]), hot_c, hot_a)
    out[:, Q:] = reorder(block(role[2]), hot_c, hot_c)


def first_inverse_kernel(s_own, s_peer, inv):
    inv[...] = s_own[...] + s_peer[...]
    invert(inv)


def level_one_kernel(role, inv, own, peer, zt, c00, mine, c01, c11):
    west = role[5] == 0
    a, b = own[...], peer[...]
    kn_w, kn_e = jnp.where(west, a, b), jnp.where(west, b, a)
    k_w, n_w, k_e, n_e = kn_w[:, :Q], kn_w[:, Q:], kn_e[:, :Q], kn_e[:, Q:]
    z_w, z_e = dot(k_w, inv[...]), dot(k_e, inv[...])
    zt[:Q, :] = z_w
    zt[Q:, :] = z_e
    c00[...] = n_w - dot_t(z_w, k_w)
    we = -dot_t(z_w, k_e)
    ee = n_e - dot_t(z_e, k_e)
    c01[...] = we
    c11[...] = ee
    mine[:Q, :] = jnp.where(west, we, ee)
    mine[Q:, :] = jnp.where(west, z_w, z_e)


def second_inverse_kernel(c_own, c_peer, inv):
    inv[...] = c_own[...] + c_peer[...]
    invert(inv)


def third_inverse_kernel(role, inv0, c01, c11, far, far_peer, gt, b_out, inv):
    west = role[5] == 0
    f, g = far[:Q, :], far_peer[:Q, :]
    b = c01[...] + jnp.where(west, f, g)
    d = c11[...] + jnp.where(west, g, f)
    b_out[...] = b
    gt[...] = dot(b.T, inv0[...])
    inv[...] = d - dot(gt[...], b)
    invert(inv)


def final_kernel(
    role, table, inv_own, from_ext, zt_own, zt_far, zt_far_peer, inv0, b, gt, inv1,
    d_own, e_own, r0, r1, r2, swapped, out, ux, up, dp, iv, x, t, zf, sem,
):
    own, core, zpos, ext = role[0], role[5], role[6], role[7]
    half = 1 - ext
    even = 1 - own % 2
    near, far = (1 - ext) * (1 - even), (1 - ext) * even
    held = (r0, r1, r2, e_own) + tuple(swapped.at[pl.ds(k * Q, Q), :] for k in range(3))
    entry = ((zpos * 2 + core) * 4 + own) * 5
    for j in range(5):
        which = table[entry + j]
        to = up if j == 4 else ux.at[j]
        for i in range(3 if j == 4 else 0, 7):
            @pl.when(which == i)
            def _(i=i, j=j, to=to):
                pltpu.make_async_copy(held[i], to, sem.at[j]).start()
    for use, refs in (
        (ext == 1, (d_own.at[:, pl.ds(0, Q)], d_own.at[:, pl.ds(Q, Q)])),
        (far == 1, (from_ext.at[pl.ds(Q, Q), :], from_ext.at[pl.ds(2 * Q, Q), :])),
        (near == 1, (swapped.at[pl.ds(3 * Q, Q), pl.ds(0, Q)], swapped.at[pl.ds(3 * Q, Q), pl.ds(Q, Q)])),
    ):
        @pl.when(use)
        def _(refs=refs):
            for k in range(2):
                pltpu.make_async_copy(refs[k], dp.at[k], sem.at[5 + k]).start()
    i_copy = pltpu.make_async_copy(from_ext.at[pl.ds(0, Q), :], iv, sem.at[7])
    i_copy.start()
    p_copy = pltpu.make_async_copy(held[3], up, sem.at[4])
    west = core == 0
    zf[:Q, :] = jnp.where(west, zt_far[Q:, :], zt_far_peer[Q:, :])
    zf[Q:, :] = jnp.where(west, zt_far_peer[Q:, :], zt_far[Q:, :])
    p_copy.wait()
    i_copy.wait()
    is_far = far == 1
    a_p, c_p = up[:, :Q], up[:, Q:]
    inv_p = jnp.where(is_far, iv[...], inv_own[...])
    zt_p = jnp.where(is_far, zf[...], zt_own[...])
    p_core = jnp.where(near == 1, 1 - core, core)
    p_zpos = jnp.where(is_far, 1 - zpos, zpos)
    y = dot(a_p, inv_p)
    v2 = -dot_t(a_p, zt_p)
    on_west = p_core == 0
    v2_w = v2[:, :Q] + jnp.where(on_west, c_p, 0.0)
    v2_e = v2[:, Q:] + jnp.where(on_west, 0.0, c_p)
    u1 = dot(v2_w, inv0[...])
    s2 = dot(v2_e - dot(u1, b[...]), inv1[...])
    s1 = u1 - dot(s2, gt[...])
    x[:, :Q] = s1
    x[:, Q:] = s2
    xs = x[...]
    own_t = dot3(xs, zt_own[...])
    far_t = dot3(xs, zf[...])
    t[0] = jnp.where(is_far, -own_t, y - own_t)
    t[1] = jnp.where(is_far, y - far_t, -far_t)
    for j in range(4):
        pltpu.make_async_copy(held[3], ux.at[j], sem.at[j]).wait()
    pairs = ((0, 1), (0, 1), (0, 0), (1, 1))
    leaves = ((0, 0), (1, 1), (1, 0), (1, 0))
    for k in range(4):
        pair = jnp.where(half == 0, pairs[k][0], pairs[k][1])
        leaf = jnp.where(half == 0, leaves[k][0], leaves[k][1])
        tk = t[jnp.where(pair == zpos, 0, 1)]
        xk = jnp.where(leaf == 0, x[:, :Q], x[:, Q:])
        out[k * Q : k * Q + Q, :] = -(dot3(ux[k, :, :Q], tk, 1) + dot3(ux[k, :, Q:], xk, 1))
    z_row = pl.ds(pl.multiple_of(p_core * Q, Q), Q)
    x_row = pl.ds(pl.multiple_of((2 + p_zpos) * Q, Q), Q)
    for k in range(2):
        pltpu.make_async_copy(d_own.at[:, pl.ds(0, Q)], dp.at[k], sem.at[5 + k]).wait()

    @pl.when(half == 1 - p_core)
    def _():
        out[x_row, :] = out[x_row, :] + dp[0]

    @pl.when(half == p_zpos)
    def _():
        out[z_row, :] = out[z_row, :] + dp[1]


def sides_of(core, zpos):
    return 1 + 2 * core, 2 - 2 * zpos, 3 - 2 * core, 2 * zpos


def pairs_of(boxes, route):
    out = []
    for k in range(boxes // 4):
        for z in range(2):
            for core in range(2):
                for col in range(4):
                    to = route(core, z, col)
                    if to is not None:
                        out.append((
                            (4 * k + 2 * z + core) * 4 + col,
                            (4 * k + 2 * to[1] + to[0]) * 4 + to[2],
                        ))
    return out


def slot_of(core, zpos, col):
    return (core, 1 - (zpos ^ core), core, zpos ^ core)[col]


def plan_rounds():
    devices = [(core, z, col) for z in range(2) for core in range(2) for col in range(4)]
    half = {d: 0 if d[2] in sides_of(d[0], d[1])[2:] else 1 for d in devices}
    edges = []
    for d in devices:
        core, z, col = d
        for c in (2 * half[d], 2 * half[d] + 1):
            for k in range(2):
                if c != col and (col % 2 == 1 or k == core):
                    source = [s for s in devices if s[1] == z and s[2] == c and slot_of(*s) == k][0]
                    early = col % 2 == 0
                    if col % 2 == 1 and col // 2 != half[d] and (c, k) == (2 * half[d] + 1, 1):
                        edges.append((source, (1 - core, z, col), (c, k), 2))
                    else:
                        edges.append((source, d, (c, k), 2 if early else 3))
    edges.sort(key=lambda e: (e[3], e))
    sends, takes = {}, {}

    def place(n):
        if n == len(edges):
            return True
        source, to, panel, limit = edges[n]
        for r in range(limit):
            if (source, r) not in sends and (to, r) not in takes:
                sends[source, r] = to
                takes[to, r] = panel
                if place(n + 1):
                    return True
                del sends[source, r], takes[to, r]
        return False

    assert place(0)
    routes = [{a: b for (a, r), b in sends.items() if r == q} for q in range(3)]
    table = []
    for d in devices:
        core, z, col = d
        sibling = (1 - core, z, col)
        for c in (2 * half[d], 2 * half[d] + 1):
            for k in range(2):
                if c == col:
                    table.append(3 if k == slot_of(*d) else 4)
                    continue
                here = [r for r in range(3) if takes.get((d, r)) == (c, k)]
                there = [5 + r for r in range(2) if takes.get((sibling, r)) == (c, k)]
                table.append((here + there)[0])
        table.append(4 if half[d] == 1 and col % 2 == 1 else 3)
    return routes, table


def body(leaf_maps, leaf_nodes):
    boxes = lax.axis_size("box")

    def send(value, route):
        return lax.ppermute(value, ("box", "col"), pairs_of(boxes, route))

    def swap_core(core, z, col):
        return 1 - core, z, col

    def swap_z(core, z, col):
        return core, 1 - z, col

    def is_ext(core, z, col):
        return col in sides_of(core, z)[2:]

    def shift_if(test, step):
        return lambda core, z, col: (core, z, (col + step) % 4) if test(core, z, col) else None

    box = lax.axis_index("box")
    col = lax.axis_index("col")
    core, zpos = box % 2, box // 2 % 2
    ia, ic, ex, ez = sides_of(core, zpos)
    ext = ((col == ex) | (col == ez)).astype(jnp.int32)
    role = jnp.stack([col, ia, ic, ex, ez, core, zpos, ext]).astype(jnp.int32)
    routes, table = plan_rounds()

    square = (Q, Q)
    panel, nodes = leaf_maps[0], leaf_nodes[0]

    def from_ia(core, z, col):
        return col == sides_of(core, z)[0]

    raw = lax.dynamic_slice(panel, (ia * Q, 0), square)
    got = [send(raw, shift_if(from_ia, s)) for s in (1, 2, 3)]
    u_part, d_part = call(permute_kernel, [(Q, 2 * Q)] * 2, [SMEM, VMEM, VMEM], 1 << 30)(role, panel, nodes)
    s_own, = call(coupling_kernel, [square], [SMEM] + [VMEM] * 5, 1 << 28)(role, raw, *got, nodes)
    s_peer = send(s_own, swap_core)

    def from_inner(core, z, col):
        return col in sides_of(core, z)[:2]

    raw = lax.dynamic_slice(panel, (ic * Q, 0), square)
    inner = [raw] + [send(raw, shift_if(from_inner, s)) for s in (1, 2, 3)]

    def spread(core, z, col):
        if not is_ext(core, z, col):
            return None
        return (core, 1 - z, col) if col % 2 == 0 else (1 - core, 1 - z, col)

    e_own = jnp.where(ext == 1, u_part, send(u_part, spread))

    def to_far_inner(core, z, col):
        return (core, 1 - z, col) if is_ext(core, z, col) and col % 2 == 0 else None

    inv_own, = call(first_inverse_kernel, [square], [VMEM] * 2, 10 << 30)(s_own, s_peer)

    kn_own, = call(inner_kernel, [(Q, 2 * Q)], [SMEM] + [VMEM] * 5, 1 << 28)(role, *inner, nodes)
    kn_peer = send(kn_own, swap_core)
    rounds = [send(e_own, lambda *d, r=r: routes[r].get(d)) for r in range(3)]
    swapped = send(jnp.concatenate([e_own, rounds[0], rounds[1], d_part], axis=0), swap_core)

    zt, c00, mine, c01, c11 = call(
        level_one_kernel, [(2 * Q, Q), square, (2 * Q, Q), square, square], [SMEM] + [VMEM] * 3, 2 << 30
    )(role, inv_own, kn_own, kn_peer)

    c00_far = send(c00, swap_z)
    mine_far = send(mine, swap_z)
    mine_far_peer = send(mine_far, swap_core)

    to_far = jnp.concatenate([inv_own, d_part[:, :Q], d_part[:, Q:]], axis=0)
    from_ext = send(to_far, to_far_inner)

    inv0, = call(second_inverse_kernel, [square], [VMEM] * 2, 10 << 30)(c00, c00_far)
    gt, b, inv1 = call(
        third_inverse_kernel, [square] * 3, [SMEM] + [VMEM] * 5, 10 << 30
    )(role, inv0, c01, c11, mine_far, mine_far_peer)
    out, = call(
        final_kernel,
        [(4 * Q, Q)],
        [SMEM] * 2 + [VMEM, ANY] + [VMEM] * 7 + [ANY] * 6,
        4 << 30,
        scratch=[
            pltpu.VMEM((4, Q, 2 * Q), F32),
            pltpu.VMEM((Q, 2 * Q), F32),
            pltpu.VMEM((2, Q, Q), F32),
            pltpu.VMEM((Q, Q), F32),
            pltpu.VMEM((Q, 2 * Q), F32),
            pltpu.VMEM((2, Q, Q), F32),
            pltpu.VMEM((2 * Q, Q), F32),
            pltpu.SemaphoreType.DMA((8,)),
        ],
    )(
        role, jnp.asarray(table, dtype=jnp.int32), inv_own, from_ext, zt, mine_far, mine_far_peer, inv0, b, gt,
        inv1, d_part, e_own, *rounds, swapped,
    )
    return out[None]


def solution(mesh):
    in_specs = (P("box", None, "col"), P("box", None, None))
    out_specs = P("box", None, "col")
    return jax.shard_map(body, mesh=mesh, in_specs=in_specs, out_specs=out_specs, check_vma=False)
```

profile of v0, /device:TPU:2, one launch (start us, length us, event | category | flops | bytes accessed | tf_op | source)
XLA Modules:
  0.0 96.2 jit_solution(17071477428497805670)
XLA Ops:
  0.0 1.1 %dynamic-slice_bitcast_fusion = (f32[256,256]{1,0:T(8,128)S(1)}, f32[256,256]{1,0:T(8,128)S(1)}) fusion(f32[1,1024,256]{2,1,0:T(8,128)} %param.3, s32[]{:T(128)S(6)} %select_n.33, s32[]{:T(128)S(6)} %select_n.32), kind=kLoop, calls=%fused_computation.2 | loop fusion | bytes 1048584 | tf_op jit(solution)/shard_map/dynamic_slice | solution.py:448
  1.1 0.0 copy-start.2
  1.1 0.7 collective-permute-start.5
  1.8 1.3 %collective-permute-start.6 = (f32[256,256]{1,0:T(8,128)S(1)}, f32[256,256]{1,0:T(8,128)S(1)}, u32[]{:S(2)}, u32[]{:S(2)}) collective-permute-start(f32[256,256]{1,0:T(8,128)S(1)} %get-tuple-element.25.raw), channel_id=1, source_target_pairs={{1,3},{2,0},{6,4},{7,5},{8,10},{9,11},{12,14},{15,13},{17,19},{18,... | collective-permute-start | bytes 786440 | tf_op jit(solution)/shard_map/ppermute | solution.py:411
  3.1 0.1 stack.35.role
  3.2 1.2 %copy-done = f32[1,1024,256]{2,1,0:T(8,128)S(1)} copy-done((f32[1,1024,256]{2,1,0:T(8,128)S(1)}, f32[1,1024,256]{2,1,0:T(8,128)}, u32[]{:S(2)}) %copy-start) | copy-done | bytes 1048600
  4.4 0.7 copy-done.1
  5.1 2.2 %shard_map.39 = (f32[256,512]{1,0:T(8,128)S(1)}, f32[256,512]{1,0:T(8,128)S(1)}) custom-call(s32[8]{0:T(128)S(1)} %stack.35.role, f32[1024,256]{1,0:T(8,128)S(1)} %bitcast.15, s32[4,256]{1,0:T(4,128)S(1)} %bitcast.16), custom_call_target="tpu_custom_call" | custom-call | flops 1073741824 | bytes 1048576 | tf_op jit(solution)/shard_map/pallas_call | solution.py:441
  7.3 9.1 %collective-permute-start.12 = (f32[256,512]{1,0:T(8,128)S(1)}, f32[256,512]{1,0:T(8,128)}, u32[]{:S(2)}, u32[]{:S(2)}) collective-permute-start(f32[256,512]{1,0:T(8,128)S(1)} %get-tuple-element.24), channel_id=1, source_target_pairs={{0,8},{3,15},{4,12},{5,9},{10,2},{11,7},{13,1},{14,6},{16,24},{19,... | collective-permute-start | bytes 1572872 | tf_op jit(solution)/shard_map/ppermute | solution.py:411
  16.4 1.3 %collective-permute-start.7 = (f32[256,256]{1,0:T(8,128)S(1)}, f32[256,256]{1,0:T(8,128)S(1)}, u32[]{:S(2)}, u32[]{:S(2)}) collective-permute-start(f32[256,256]{1,0:T(8,128)S(1)} %get-tuple-element.25.raw), channel_id=1, source_target_pairs={{1,0},{2,1},{6,5},{7,6},{8,11},{9,8},{12,15},{15,14},{17,16},{18,1... | collective-permute-start | bytes 786440 | tf_op jit(solution)/shard_map/ppermute | solution.py:411
  17.6 0.7 collective-permute-start
  18.3 0.0 collective-permute-done.5.g1
  18.3 0.7 collective-permute-start.1
  19.0 0.1 collective-permute-done.6.g2
  19.1 1.3 %collective-permute-start.2 = (f32[256,256]{1,0:T(8,128)S(1)}, f32[256,256]{1,0:T(8,128)S(1)}, u32[]{:S(2)}, u32[]{:S(2)}) collective-permute-start(f32[256,256]{1,0:T(8,128)S(1)} %get-tuple-element.26.raw), channel_id=1, source_target_pairs={{1,0},{7,6},{9,8},{15,14},{17,16},{23,22},{25,24},{31,30},{33,32},... | collective-permute-start | bytes 786440 | tf_op jit(solution)/shard_map/ppermute | solution.py:411
  20.4 4.2 %collective-permute-done.7.g3 = f32[256,256]{1,0:T(8,128)S(1)} collective-permute-done((f32[256,256]{1,0:T(8,128)S(1)}, f32[256,256]{1,0:T(8,128)S(1)}, u32[]{:S(2)}, u32[]{:S(2)}) %collective-permute-start.7) | collective-permute-done | bytes 262176 | tf_op jit(solution)/shard_map/ppermute | solution.py:411
  24.6 1.6 %shard_map.40.own = f32[256,512]{1,0:T(8,128)S(1)} custom-call(s32[8]{0:T(128)S(1)} %stack.35.role, f32[256,256]{1,0:T(8,128)S(1)} %get-tuple-element.25.raw, f32[256,256]{1,0:T(8,128)S(1)} %collective-permute-done.5.g1, f32[256,256]{1,0:T(8,128)S(1)} %collective-permute-done.6.g2, f32[256,256]{1,0:T(8,128)S(1)} %collective-permute-done.7.g3, ...), custom_call_target="tpu_custom_call" | custom-call | flops 268435456 | bytes 1048576 | tf_op jit(solution)/shard_map/pallas_call | solution.py:463
  26.2 0.1 collective-permute-start.8
  26.3 0.0 collective-permute-done.g1
  26.4 0.0 collective-permute-done.1.g2
  26.4 3.9 %collective-permute-done.2.g3 = f32[256,256]{1,0:T(8,128)S(1)} collective-permute-done((f32[256,256]{1,0:T(8,128)S(1)}, f32[256,256]{1,0:T(8,128)S(1)}, u32[]{:S(2)}, u32[]{:S(2)}) %collective-permute-start.2) | collective-permute-done | bytes 262176 | tf_op jit(solution)/shard_map/ppermute | solution.py:411
  30.2 1.2 %shard_map.37.s_own = f32[256,256]{1,0:T(8,128)S(1)} custom-call(s32[8]{0:T(128)S(1)} %stack.35.role, f32[256,256]{1,0:T(8,128)S(1)} %get-tuple-element.26.raw, f32[256,256]{1,0:T(8,128)S(1)} %collective-permute-done.g1, f32[256,256]{1,0:T(8,128)S(1)} %collective-permute-done.1.g2, f32[256,256]{1,0:T(8,128)S(1)} %collective-permute-done.2.g3, ...), custom_call_target="tpu_custom_call" | custom-call | flops 268435456 | bytes 1048576 | tf_op jit(solution)/shard_map/pallas_call | solution.py:442
  31.4 0.1 collective-permute-start.3
  31.5 0.0 collective-permute-done.12
  31.5 0.1 broadcast_select_fusion.e_own
  31.6 1.9 %collective-permute-start.13 = (f32[256,512]{1,0:T(8,128)S(1)}, f32[256,512]{1,0:T(8,128)S(1)}, u32[]{:S(2)}, u32[]{:S(2)}) collective-permute-start(f32[256,512]{1,0:T(8,128)S(1)} %broadcast_select_fusion.e_own), channel_id=1, source_target_pairs={{0,3},{1,4},{2,1},{3,2},{5,0},{6,7},{7,5},{8,10},{9,11},{10,8},{11... | collective-permute-start | bytes 1572872 | tf_op jit(solution)/shard_map/ppermute | solution.py:411
  33.5 3.9 %collective-permute-start.14 = (f32[256,512]{1,0:T(8,128)S(1)}, f32[256,512]{1,0:T(8,128)S(1)}, u32[]{:S(2)}, u32[]{:S(2)}) collective-permute-start(f32[256,512]{1,0:T(8,128)S(1)} %broadcast_select_fusion.e_own), channel_id=1, source_target_pairs={{0,5},{1,7},{3,1},{4,3},{7,6},{8,11},{9,10},{10,9},{11,13},{12,14}... | collective-permute-start | bytes 1572872 | tf_op jit(solution)/shard_map/ppermute | solution.py:411
  37.4 0.0 collective-permute-done.3.s_peer
  37.4 9.5 %shard_map.38.inv.inv_own = f32[256,256]{1,0:T(8,128)S(1)} custom-call(f32[256,256]{1,0:T(8,128)S(1)} %shard_map.37.s_own, f32[256,256]{1,0:T(8,128)S(1)} %collective-permute-done.3.s_peer), custom_call_target="tpu_custom_call" | custom-call | flops 10737418240 | bytes 1048576 | tf_op jit(solution)/shard_map/pallas_call | solution.py:461
  47.0 0.0 collective-permute-done.8.peer
  47.0 1.9 %shard_map.41 = (f32[512,256]{1,0:T(8,128)S(1)}, f32[256,256]{1,0:T(8,128)S(1)}, f32[512,256]{1,0:T(8,128)S(1)}, f32[256,256]{1,0:T(8,128)S(1)}, f32[256,256]{1,0:T(8,128)S(1)}) custom-call(s32[8]{0:T(128)S(1)} %stack.35.role, f32[256,256]{1,0:T(8,128)S(1)} %shard_map.38.inv.inv_own, f32[256,512]{1,0:T(8,128)S(1)} %shard_map.40.own, ...), custom_call_target="tpu_custom_call" | custom-call | flops 2147483648 | bytes 1048576 | tf_op jit(solution)/shard_map/pallas_call | solution.py:468
  48.8 1.3 %collective-permute-start.9 = (f32[512,256]{1,0:T(8,128)S(1)}, f32[512,256]{1,0:T(8,128)S(1)}, u32[]{:S(2)}, u32[]{:S(2)}) collective-permute-start(f32[512,256]{1,0:T(8,128)S(1)} %get-tuple-element.17), channel_id=1, source_target_pairs={{0,8},{1,9},{2,10},{3,11},{4,12},{5,13},{6,14},{7,15},{8,0},{9,1},... | collective-permute-start | bytes 1572872 | tf_op jit(solution)/shard_map/ppermute | solution.py:411
  50.2 0.7 collective-permute-start.15
  50.9 1.5 %collective-permute-start.11 = (f32[256,256]{1,0:T(8,128)S(1)}, f32[256,256]{1,0:T(8,128)S(1)}, u32[]{:S(2)}, u32[]{:S(2)}) collective-permute-start(f32[256,256]{1,0:T(8,128)S(1)} %get-tuple-element.18.c_own), channel_id=1, source_target_pairs={{0,8},{1,9},{2,10},{3,11},{4,12},{5,13},{6,14},{7,15},{8,0},{9,1},... | collective-permute-start | bytes 786440 | tf_op jit(solution)/shard_map/ppermute | solution.py:411
  52.4 0.0 collective-permute-done.13.r0
  52.4 0.2 pad_maximum_fusion
  52.6 3.5 %collective-permute-start.16 = (f32[1024,512]{1,0:T(8,128)S(1)}, f32[1024,512]{1,0:T(8,128)S(1)}, u32[]{:S(2)}, u32[]{:S(2)}) collective-permute-start(f32[1024,512]{1,0:T(8,128)S(1)} %pad_maximum_fusion), channel_id=1, source_target_pairs={{0,4},{1,5},{2,6},{3,7},{4,0},{5,1},{6,2},{7,3},{8,12},{9,13},{10,... | collective-permute-start | bytes 6291464 | tf_op jit(solution)/shard_map/ppermute | solution.py:411
  56.1 0.1 pad_maximum_fusion.1
  56.2 6.6 %collective-permute-start.4 = (f32[768,256]{1,0:T(8,128)S(1)}, f32[768,256]{1,0:T(8,128)S(1)}, u32[]{:S(2)}, u32[]{:S(2)}) collective-permute-start(f32[768,256]{1,0:T(8,128)S(1)} %pad_maximum_fusion.1), channel_id=1, source_target_pairs={{0,8},{4,12},{10,2},{14,6},{16,24},{20,28},{26,18},{30,22},{32,40}... | collective-permute-start | bytes 2359304 | tf_op jit(solution)/shard_map/ppermute | solution.py:411
  62.8 0.9 collective-permute-done.9.far.zt_far
  63.7 0.0 collective-permute-start.10
  63.7 5.0 %collective-permute-done.11.c_peer = f32[256,256]{1,0:T(8,128)S(1)} collective-permute-done((f32[256,256]{1,0:T(8,128)S(1)}, f32[256,256]{1,0:T(8,128)S(1)}, u32[]{:S(2)}, u32[]{:S(2)}) %collective-permute-start.11) | collective-permute-done | bytes 262176 | tf_op jit(solution)/shard_map/ppermute | solution.py:411
  68.7 9.6 %shard_map.42.inv0 = f32[256,256]{1,0:T(8,128)S(1)} custom-call(f32[256,256]{1,0:T(8,128)S(1)} %get-tuple-element.18.c_own, f32[256,256]{1,0:T(8,128)S(1)} %collective-permute-done.11.c_peer), custom_call_target="tpu_custom_call" | custom-call | flops 10737418240 | bytes 1048576 | tf_op jit(solution)/shard_map/pallas_call | solution.py:479
  78.3 0.0 copy-start.3
  78.3 11.3 %shard_map.43 = (f32[256,256]{1,0:T(8,128)S(1)}, f32[256,256]{1,0:T(8,128)S(1)}, f32[256,256]{1,0:T(8,128)S(1)}) custom-call(s32[8]{0:T(128)S(1)} %stack.35.role, f32[256,256]{1,0:T(8,128)S(1)} %shard_map.42.inv0, f32[256,256]{1,0:T(8,128)S(1)} %get-tuple-element.19.c01, f32[256,256]{1,0:T(8,128)S(1)} %get-tuple-element.20.c11, ...), custom_call_target="tpu_custom_call" | custom-call | flops 10737418240 | bytes 1048576 | tf_op jit(solution)/shard_map/pallas_call | solution.py:480
  89.6 0.0 collective-permute-done.15.r2
  89.6 0.0 collective-permute-done.16.swapped
  89.6 6.4 %shard_map.44 = f32[1024,256]{1,0:T(8,128)} custom-call(s32[8]{0:T(128)S(1)} %stack.35.role, s32[80]{0:T(128)S(1)} %copy-done.3, f32[256,256]{1,0:T(8,128)S(1)} %shard_map.38.inv.inv_own, f32[768,256]{1,0:T(8,128)S(1)} %collective-permute-done.4.from_ext, f32[512,256]{1,0:T(8,128)S(1)} %get-tuple-element.16.zt_own, ...), custom_call_target="tpu_custom_call" | custom-call | flops 4294967296 | bytes 1048576 | tf_op jit(solution)/shard_map/pallas_call | solution.py:483
  (8 shorter events, 0.0 us)
Async XLA Ops:
  1.1 23.5 %copy-start.2 = (s32[1,4,256]{2,1,0:T(4,128)S(1)}, s32[1,4,256]{2,1,0:T(4,128)}, u32[]{:S(2)}) copy-start(s32[1,4,256]{2,1,0:T(4,128)} %param.4) | copy-start | bytes 12292
  1.1 17.2 %collective-permute-start.5 = (f32[256,256]{1,0:T(8,128)S(1)}, f32[256,256]{1,0:T(8,128)S(1)}, u32[]{:S(2)}, u32[]{:S(2)}) collective-permute-start(f32[256,256]{1,0:T(8,128)S(1)} %get-tuple-element.25.raw), channel_id=1, source_target_pairs={{1,2},{2,3},{6,7},{7,4},{8,9},{9,10},{12,13},{15,12},{17,18},{18,1... | collective-permute-start | bytes 786440 | tf_op jit(solution)/shard_map/ppermute | solution.py:411
  1.8 17.3 %collective-permute-start.6 = (f32[256,256]{1,0:T(8,128)S(1)}, f32[256,256]{1,0:T(8,128)S(1)}, u32[]{:S(2)}, u32[]{:S(2)}) collective-permute-start(f32[256,256]{1,0:T(8,128)S(1)} %get-tuple-element.25.raw), channel_id=1, source_target_pairs={{1,3},{2,0},{6,4},{7,5},{8,10},{9,11},{12,14},{15,13},{17,19},{18,... | collective-permute-start | bytes 786440 | tf_op jit(solution)/shard_map/ppermute | solution.py:411
  3.2 1.2 %copy-start = (f32[1,1024,256]{2,1,0:T(8,128)S(1)}, f32[1,1024,256]{2,1,0:T(8,128)}, u32[]{:S(2)}) copy-start(f32[1,1024,256]{2,1,0:T(8,128)} %param.3) | copy-start | bytes 3145732
  4.4 0.7 copy-start.1
  7.3 24.2 %collective-permute-start.12 = (f32[256,512]{1,0:T(8,128)S(1)}, f32[256,512]{1,0:T(8,128)}, u32[]{:S(2)}, u32[]{:S(2)}) collective-permute-start(f32[256,512]{1,0:T(8,128)S(1)} %get-tuple-element.24), channel_id=1, source_target_pairs={{0,8},{3,15},{4,12},{5,9},{10,2},{11,7},{13,1},{14,6},{16,24},{19,... | collective-permute-start | bytes 1572872 | tf_op jit(solution)/shard_map/ppermute | solution.py:411
  16.4 8.3 %collective-permute-start.7 = (f32[256,256]{1,0:T(8,128)S(1)}, f32[256,256]{1,0:T(8,128)S(1)}, u32[]{:S(2)}, u32[]{:S(2)}) collective-permute-start(f32[256,256]{1,0:T(8,128)S(1)} %get-tuple-element.25.raw), channel_id=1, source_target_pairs={{1,0},{2,1},{6,5},{7,6},{8,11},{9,8},{12,15},{15,14},{17,16},{18,1... | collective-permute-start | bytes 786440 | tf_op jit(solution)/shard_map/ppermute | solution.py:411
  17.6 8.7 %collective-permute-start = (f32[256,256]{1,0:T(8,128)S(1)}, f32[256,256]{1,0:T(8,128)S(1)}, u32[]{:S(2)}, u32[]{:S(2)}) collective-permute-start(f32[256,256]{1,0:T(8,128)S(1)} %get-tuple-element.26.raw), channel_id=1, source_target_pairs={{1,2},{7,4},{9,10},{15,12},{17,18},{23,20},{25,26},{31,28},{33,34}... | collective-permute-start | bytes 786440 | tf_op jit(solution)/shard_map/ppermute | solution.py:411
  18.3 8.0 %collective-permute-start.1 = (f32[256,256]{1,0:T(8,128)S(1)}, f32[256,256]{1,0:T(8,128)S(1)}, u32[]{:S(2)}, u32[]{:S(2)}) collective-permute-start(f32[256,256]{1,0:T(8,128)S(1)} %get-tuple-element.26.raw), channel_id=1, source_target_pairs={{1,3},{7,5},{9,11},{15,13},{17,19},{23,21},{25,27},{31,29},{33,35}... | collective-permute-start | bytes 786440 | tf_op jit(solution)/shard_map/ppermute | solution.py:411
  19.1 11.1 %collective-permute-start.2 = (f32[256,256]{1,0:T(8,128)S(1)}, f32[256,256]{1,0:T(8,128)S(1)}, u32[]{:S(2)}, u32[]{:S(2)}) collective-permute-start(f32[256,256]{1,0:T(8,128)S(1)} %get-tuple-element.26.raw), channel_id=1, source_target_pairs={{1,0},{7,6},{9,8},{15,14},{17,16},{23,22},{25,24},{31,30},{33,32},... | collective-permute-start | bytes 786440 | tf_op jit(solution)/shard_map/ppermute | solution.py:411
  26.2 20.7 %collective-permute-start.8 = (f32[256,512]{1,0:T(8,128)S(1)}, f32[256,512]{1,0:T(8,128)S(1)}, u32[]{:S(2)}, u32[]{:S(2)}) collective-permute-start(f32[256,512]{1,0:T(8,128)S(1)} %shard_map.40.own), channel_id=1, source_target_pairs={{0,4},{1,5},{2,6},{3,7},{4,0},{5,1},{6,2},{7,3},{8,12},{9,13},{10,... | collective-permute-start | bytes 1572872 | tf_op jit(solution)/shard_map/ppermute | solution.py:411
  31.4 6.0 %collective-permute-start.3 = (f32[256,256]{1,0:T(8,128)S(1)}, f32[256,256]{1,0:T(8,128)S(1)}, u32[]{:S(2)}, u32[]{:S(2)}) collective-permute-start(f32[256,256]{1,0:T(8,128)S(1)} %shard_map.37.s_own), channel_id=1, source_target_pairs={{0,4},{1,5},{2,6},{3,7},{4,0},{5,1},{6,2},{7,3},{8,12},{9,13},{10,... | collective-permute-start | bytes 786440 | tf_op jit(solution)/shard_map/ppermute | solution.py:411
  31.6 20.8 %collective-permute-start.13 = (f32[256,512]{1,0:T(8,128)S(1)}, f32[256,512]{1,0:T(8,128)S(1)}, u32[]{:S(2)}, u32[]{:S(2)}) collective-permute-start(f32[256,512]{1,0:T(8,128)S(1)} %broadcast_select_fusion.e_own), channel_id=1, source_target_pairs={{0,3},{1,4},{2,1},{3,2},{5,0},{6,7},{7,5},{8,10},{9,11},{10,8},{11... | collective-permute-start | bytes 1572872 | tf_op jit(solution)/shard_map/ppermute | solution.py:411
  33.5 18.9 %collective-permute-start.14 = (f32[256,512]{1,0:T(8,128)S(1)}, f32[256,512]{1,0:T(8,128)S(1)}, u32[]{:S(2)}, u32[]{:S(2)}) collective-permute-start(f32[256,512]{1,0:T(8,128)S(1)} %broadcast_select_fusion.e_own), channel_id=1, source_target_pairs={{0,5},{1,7},{3,1},{4,3},{7,6},{8,11},{9,10},{10,9},{11,13},{12,14}... | collective-permute-start | bytes 1572872 | tf_op jit(solution)/shard_map/ppermute | solution.py:411
  48.8 14.9 %collective-permute-start.9 = (f32[512,256]{1,0:T(8,128)S(1)}, f32[512,256]{1,0:T(8,128)S(1)}, u32[]{:S(2)}, u32[]{:S(2)}) collective-permute-start(f32[512,256]{1,0:T(8,128)S(1)} %get-tuple-element.17), channel_id=1, source_target_pairs={{0,8},{1,9},{2,10},{3,11},{4,12},{5,13},{6,14},{7,15},{8,0},{9,1},... | collective-permute-start | bytes 1572872 | tf_op jit(solution)/shard_map/ppermute | solution.py:411
  50.2 39.4 %collective-permute-start.15 = (f32[256,512]{1,0:T(8,128)S(1)}, f32[256,512]{1,0:T(8,128)S(1)}, u32[]{:S(2)}, u32[]{:S(2)}) collective-permute-start(f32[256,512]{1,0:T(8,128)S(1)} %broadcast_select_fusion.e_own), channel_id=1, source_target_pairs={{2,7},{4,5},{5,3},{6,1},{8,13},{10,15},{12,11},{14,9},{18,23},{20,... | collective-permute-start | bytes 1572872 | tf_op jit(solution)/shard_map/ppermute | solution.py:411
  50.9 17.8 %collective-permute-start.11 = (f32[256,256]{1,0:T(8,128)S(1)}, f32[256,256]{1,0:T(8,128)S(1)}, u32[]{:S(2)}, u32[]{:S(2)}) collective-permute-start(f32[256,256]{1,0:T(8,128)S(1)} %get-tuple-element.18.c_own), channel_id=1, source_target_pairs={{0,8},{1,9},{2,10},{3,11},{4,12},{5,13},{6,14},{7,15},{8,0},{9,1},... | collective-permute-start | bytes 786440 | tf_op jit(solution)/shard_map/ppermute | solution.py:411
  52.6 37.0 %collective-permute-start.16 = (f32[1024,512]{1,0:T(8,128)S(1)}, f32[1024,512]{1,0:T(8,128)S(1)}, u32[]{:S(2)}, u32[]{:S(2)}) collective-permute-start(f32[1024,512]{1,0:T(8,128)S(1)} %pad_maximum_fusion), channel_id=1, source_target_pairs={{0,4},{1,5},{2,6},{3,7},{4,0},{5,1},{6,2},{7,3},{8,12},{9,13},{10,... | collective-permute-start | bytes 6291464 | tf_op jit(solution)/shard_map/ppermute | solution.py:411
  56.2 33.4 %collective-permute-start.4 = (f32[768,256]{1,0:T(8,128)S(1)}, f32[768,256]{1,0:T(8,128)S(1)}, u32[]{:S(2)}, u32[]{:S(2)}) collective-permute-start(f32[768,256]{1,0:T(8,128)S(1)} %pad_maximum_fusion.1), channel_id=1, source_target_pairs={{0,8},{4,12},{10,2},{14,6},{16,24},{20,28},{26,18},{30,22},{32,40}... | collective-permute-start | bytes 2359304 | tf_op jit(solution)/shard_map/ppermute | solution.py:411
  63.7 14.5 %collective-permute-start.10 = (f32[512,256]{1,0:T(8,128)S(1)}, f32[512,256]{1,0:T(8,128)S(1)}, u32[]{:S(2)}, u32[]{:S(2)}) collective-permute-start(f32[512,256]{1,0:T(8,128)S(1)} %collective-permute-done.9.far.zt_far), channel_id=1, source_target_pairs={{0,4},{1,5},{2,6},{3,7},{4,0},{5,1},{6,2},{7,3},{8,12},{9,13},{10,... | collective-permute-start | bytes 1572872 | tf_op jit(solution)/shard_map/ppermute | solution.py:411
  78.3 11.4 %copy-start.3 = (s32[80]{0:T(128)S(1)}, s32[80]{0:T(128)}, u32[]{:S(2)}) copy-start(s32[80]{0:T(128)} %constant.49.clone.table) | copy-start | bytes 964
where the time goes:
time: 97.5 us; the launch traced here: 96.2 us
  Pallas kernels  43.6 us (45%)
  starting transfers between devices  34.6 us (35%)
  waiting for transfers between devices  14.1 us (14%)
  local copies, waits for them, and re-layouts  3.11 us (3%)
    ppermute x17, starting transfers between devices, send(): return lax.ppermute(value, ('box', 'col'), pairs_of(boxes, route))  34.6 us
    ppermute x17, waiting for transfers between devices, send(): return lax.ppermute(value, ('box', 'col'), pairs_of(boxes, route))  14.1 us
    pallas_call x1, Pallas kernels, body(): call(third_inverse_kernel, [square] * 3, [SMEM] + [VMEM] * 5, 10 << 30)  11.3 us
    pallas_call x1, Pallas kernels, body(): call(second_inverse_kernel, [square], [VMEM] * 2, 10 << 30)(c00, c00_far)  9.55 us
    pallas_call x1, Pallas kernels, body(): call(first_inverse_kernel, [square], [VMEM] * 2, 10 << 30)(s_own, s_peer)  9.54 us
    pallas_call x1, Pallas kernels, body(): call(final_kernel, [(4 * Q, Q)], [SMEM] * 2 + [VMEM, ANY] + [VMEM] * 7 +...  6.38 us
    pallas_call x1, Pallas kernels, body(): call(permute_kernel, [(Q, 2 * Q)] * 2, [SMEM, VMEM, VMEM], 1 << 30)  2.19 us
  transfers between devices with their start and end apart: 17, of which 5 were waited for; matrix products, arithmetic and copies ran while one was open for 0% of the time, Pallas kernels for 39%

commit v1 on v0

--- a/solution.py
+++ b/solution.py
@@ -220,7 +220,7 @@
     invert(inv)
 
 
-def level_one_kernel(role, inv, own, peer, zt, c00, mine, c01, c11):
+def level_one_kernel(role, inv, own, peer, zt, c00, c00_half, mine, c01, c11):
     west = role[5] == 0
     a, b = own[...], peer[...]
     kn_w, kn_e = jnp.where(west, a, b), jnp.where(west, b, a)
@@ -228,7 +228,9 @@
     z_w, z_e = dot(k_w, inv[...]), dot(k_e, inv[...])
     zt[:Q, :] = z_w
     zt[Q:, :] = z_e
-    c00[...] = n_w - dot_t(z_w, k_w)
+    ww = n_w - dot_t(z_w, k_w)
+    c00[...] = ww
+    c00_half[...] = jnp.where(west, ww[: Q // 2], ww[Q // 2 :])
     we = -dot_t(z_w, k_e)
     ee = n_e - dot_t(z_e, k_e)
     c01[...] = we
@@ -237,8 +239,11 @@
     mine[Q:, :] = jnp.where(west, z_w, z_e)
 
 
-def second_inverse_kernel(c_own, c_peer, inv):
-    inv[...] = c_own[...] + c_peer[...]
+def second_inverse_kernel(role, c_own, far, far_peer, inv):
+    west = role[5] == 0
+    f, g = far[...], far_peer[...]
+    inv[: Q // 2, :] = c_own[: Q // 2, :] + jnp.where(west, f, g)
+    inv[Q // 2 :, :] = c_own[Q // 2 :, :] + jnp.where(west, g, f)
     invert(inv)
 
 
@@ -254,42 +259,35 @@
 
 
 def final_kernel(
-    role, table, inv_own, from_ext, zt_own, zt_far, zt_far_peer, inv0, b, gt, inv1,
-    d_own, e_own, r0, r1, r2, swapped, out, ux, up, dp, iv, x, t, zf, sem,
+    role, table, inv_own, inv_far, zt_own, zt_far, zt_far_peer, inv0, b, gt, inv1,
+    d_own, d_far, e_own, r0, r1, r2, swapped, out, ux, up, dp, x, t, zf, sem,
 ):
     own, core, zpos, ext = role[0], role[5], role[6], role[7]
     half = 1 - ext
     even = 1 - own % 2
     near, far = (1 - ext) * (1 - even), (1 - ext) * even
-    held = (r0, r1, r2, e_own) + tuple(swapped.at[pl.ds(k * Q, Q), :] for k in range(3))
+    held = (r0, r1, r2, e_own) + tuple(swapped.at[pl.ds(k * Q, Q), :] for k in range(4))
     entry = ((zpos * 2 + core) * 4 + own) * 5
     for j in range(5):
         which = table[entry + j]
         to = up if j == 4 else ux.at[j]
-        for i in range(3 if j == 4 else 0, 7):
+        for i in range(3 if j == 4 else 0, 8):
             @pl.when(which == i)
             def _(i=i, j=j, to=to):
                 pltpu.make_async_copy(held[i], to, sem.at[j]).start()
-    for use, refs in (
-        (ext == 1, (d_own.at[:, pl.ds(0, Q)], d_own.at[:, pl.ds(Q, Q)])),
-        (far == 1, (from_ext.at[pl.ds(Q, Q), :], from_ext.at[pl.ds(2 * Q, Q), :])),
-        (near == 1, (swapped.at[pl.ds(3 * Q, Q), pl.ds(0, Q)], swapped.at[pl.ds(3 * Q, Q), pl.ds(Q, Q)])),
-    ):
+    for use, ref in ((ext == 1, d_own), (ext == 0, d_far)):
         @pl.when(use)
-        def _(refs=refs):
+        def _(ref=ref):
             for k in range(2):
-                pltpu.make_async_copy(refs[k], dp.at[k], sem.at[5 + k]).start()
-    i_copy = pltpu.make_async_copy(from_ext.at[pl.ds(0, Q), :], iv, sem.at[7])
-    i_copy.start()
+                pltpu.make_async_copy(ref.at[:, pl.ds(k * Q, Q)], dp.at[k], sem.at[5 + k]).start()
     p_copy = pltpu.make_async_copy(held[3], up, sem.at[4])
     west = core == 0
     zf[:Q, :] = jnp.where(west, zt_far[Q:, :], zt_far_peer[Q:, :])
     zf[Q:, :] = jnp.where(west, zt_far_peer[Q:, :], zt_far[Q:, :])
     p_copy.wait()
-    i_copy.wait()
     is_far = far == 1
     a_p, c_p = up[:, :Q], up[:, Q:]
-    inv_p = jnp.where(is_far, iv[...], inv_own[...])
+    inv_p = jnp.where(is_far, inv_far[...], inv_own[...])
     zt_p = jnp.where(is_far, zf[...], zt_own[...])
     p_core = jnp.where(near == 1, 1 - core, core)
     p_zpos = jnp.where(is_far, 1 - zpos, zpos)
@@ -355,53 +353,22 @@
     return (core, 1 - (zpos ^ core), core, zpos ^ core)[col]
 
 
-def plan_rounds():
-    devices = [(core, z, col) for z in range(2) for core in range(2) for col in range(4)]
-    half = {d: 0 if d[2] in sides_of(d[0], d[1])[2:] else 1 for d in devices}
-    edges = []
-    for d in devices:
-        core, z, col = d
-        for c in (2 * half[d], 2 * half[d] + 1):
-            for k in range(2):
-                if c != col and (col % 2 == 1 or k == core):
-                    source = [s for s in devices if s[1] == z and s[2] == c and slot_of(*s) == k][0]
-                    early = col % 2 == 0
-                    if col % 2 == 1 and col // 2 != half[d] and (c, k) == (2 * half[d] + 1, 1):
-                        edges.append((source, (1 - core, z, col), (c, k), 2))
-                    else:
-                        edges.append((source, d, (c, k), 2 if early else 3))
-    edges.sort(key=lambda e: (e[3], e))
-    sends, takes = {}, {}
-
-    def place(n):
-        if n == len(edges):
-            return True
-        source, to, panel, limit = edges[n]
-        for r in range(limit):
-            if (source, r) not in sends and (to, r) not in takes:
-                sends[source, r] = to
-                takes[to, r] = panel
-                if place(n + 1):
-                    return True
-                del sends[source, r], takes[to, r]
-        return False
-
-    assert place(0)
-    routes = [{a: b for (a, r), b in sends.items() if r == q} for q in range(3)]
+def panel_table():
     table = []
-    for d in devices:
-        core, z, col = d
-        sibling = (1 - core, z, col)
-        for c in (2 * half[d], 2 * half[d] + 1):
-            for k in range(2):
-                if c == col:
-                    table.append(3 if k == slot_of(*d) else 4)
-                    continue
-                here = [r for r in range(3) if takes.get((d, r)) == (c, k)]
-                there = [5 + r for r in range(2) if takes.get((sibling, r)) == (c, k)]
-                table.append((here + there)[0])
-        table.append(4 if half[d] == 1 and col % 2 == 1 else 3)
-    return routes, table
+    for z in range(2):
+        for core in range(2):
+            for col in range(4):
+                half = 0 if col in sides_of(core, z)[2:] else 1
+                for c in (2 * half, 2 * half + 1):
+                    for k in range(2):
+                        mine = k == slot_of(core, z, c)
+                        if c == col:
+                            table.append(3 if mine else 4)
+                        else:
+                            swap = (col ^ 1, 3 - col, col ^ 2).index(c)
+                            table.append(swap if mine else 5 + swap)
+                table.append(4 if half == 1 and col % 2 == 1 else 3)
+    return table
 
 
 def body(leaf_maps, leaf_nodes):
@@ -415,9 +382,6 @@
 
     def swap_z(core, z, col):
         return core, 1 - z, col
-
-    def is_ext(core, z, col):
-        return col in sides_of(core, z)[2:]
 
     def shift_if(test, step):
         return lambda core, z, col: (core, z, (col + step) % 4) if test(core, z, col) else None
@@ -428,7 +392,7 @@
     ia, ic, ex, ez = sides_of(core, zpos)
     ext = ((col == ex) | (col == ez)).astype(jnp.int32)
     role = jnp.stack([col, ia, ic, ex, ez, core, zpos, ext]).astype(jnp.int32)
-    routes, table = plan_rounds()
+    table = panel_table()
 
     square = (Q, Q)
     panel, nodes = leaf_maps[0], leaf_nodes[0]
@@ -449,55 +413,58 @@
     inner = [raw] + [send(raw, shift_if(from_inner, s)) for s in (1, 2, 3)]
 
     def spread(core, z, col):
-        if not is_ext(core, z, col):
-            return None
         return (core, 1 - z, col) if col % 2 == 0 else (1 - core, 1 - z, col)
 
     e_own = jnp.where(ext == 1, u_part, send(u_part, spread))
 
-    def to_far_inner(core, z, col):
-        return (core, 1 - z, col) if is_ext(core, z, col) and col % 2 == 0 else None
+    def to_inner(core, z, col):
+        return (core, 1 - z, col) if col % 2 == 0 else (1 - core, z, col)
 
     inv_own, = call(first_inverse_kernel, [square], [VMEM] * 2, 10 << 30)(s_own, s_peer)
 
     kn_own, = call(inner_kernel, [(Q, 2 * Q)], [SMEM] + [VMEM] * 5, 1 << 28)(role, *inner, nodes)
     kn_peer = send(kn_own, swap_core)
-    rounds = [send(e_own, lambda *d, r=r: routes[r].get(d)) for r in range(3)]
-    swapped = send(jnp.concatenate([e_own, rounds[0], rounds[1], d_part], axis=0), swap_core)
-
-    zt, c00, mine, c01, c11 = call(
-        level_one_kernel, [(2 * Q, Q), square, (2 * Q, Q), square, square], [SMEM] + [VMEM] * 3, 2 << 30
+    swaps = (
+        lambda core, z, col: (core, z, col ^ 1),
+        lambda core, z, col: (core, z, 3 - col),
+        lambda core, z, col: (1 - core, z, col) if z == 0 and col % 2 == 0 else (core, z, col ^ 2),
+    )
+    rounds = [send(e_own, route) for route in swaps]
+    swapped = send(jnp.concatenate([e_own, *rounds], axis=0), swap_core)
+
+    zt, c00, c00_half, mine, c01, c11 = call(
+        level_one_kernel, [(2 * Q, Q), square, (Q // 2, Q), (2 * Q, Q), square, square], [SMEM] + [VMEM] * 3, 2 << 30
     )(role, inv_own, kn_own, kn_peer)
 
-    c00_far = send(c00, swap_z)
+    c00_far = send(c00_half, swap_z)
+    c00_far_peer = send(c00_far, swap_core)
     mine_far = send(mine, swap_z)
     mine_far_peer = send(mine_far, swap_core)
 
-    to_far = jnp.concatenate([inv_own, d_part[:, :Q], d_part[:, Q:]], axis=0)
-    from_ext = send(to_far, to_far_inner)
-
-    inv0, = call(second_inverse_kernel, [square], [VMEM] * 2, 10 << 30)(c00, c00_far)
+    d_far = send(d_part, to_inner)
+    inv_far = send(inv_own, to_inner)
+
+    inv0, = call(second_inverse_kernel, [square], [SMEM] + [VMEM] * 3, 10 << 30)(role, c00, c00_far, c00_far_peer)
     gt, b, inv1 = call(
         third_inverse_kernel, [square] * 3, [SMEM] + [VMEM] * 5, 10 << 30
     )(role, inv0, c01, c11, mine_far, mine_far_peer)
     out, = call(
         final_kernel,
         [(4 * Q, Q)],
-        [SMEM] * 2 + [VMEM, ANY] + [VMEM] * 7 + [ANY] * 6,
+        [SMEM] * 2 + [VMEM] * 9 + [ANY] * 7,
         4 << 30,
         scratch=[
             pltpu.VMEM((4, Q, 2 * Q), F32),
             pltpu.VMEM((Q, 2 * Q), F32),
             pltpu.VMEM((2, Q, Q), F32),
-            pltpu.VMEM((Q, Q), F32),
             pltpu.VMEM((Q, 2 * Q), F32),
             pltpu.VMEM((2, Q, Q), F32),
             pltpu.VMEM((2 * Q, Q), F32),
-            pltpu.SemaphoreType.DMA((8,)),
+            pltpu.SemaphoreType.DMA((7,)),
         ],
     )(
-        role, jnp.asarray(table, dtype=jnp.int32), inv_own, from_ext, zt, mine_far, mine_far_peer, inv0, b, gt,
-        inv1, d_part, e_own, *rounds, swapped,
+        role, jnp.asarray(table, dtype=jnp.int32), inv_own, inv_far, zt, mine_far, mine_far_peer, inv0, b, gt,
+        inv1, d_part, d_far, e_own, *rounds, swapped,
     )
     return out[None]
 

time: 97.5 us -> 93.3 us (0.957)
  starting transfers between devices: 34.6 us -> 20.6 us
  waiting for transfers between devices: 14.1 us -> 22.9 us
    ppermute x17 -> x19, starting transfers between devices: 34.6 us -> 20.6 us  [send(): return lax.ppermute(value, ('box', 'col'), pairs_of(boxes, route))]
    ppermute x17 -> x19, waiting for transfers between devices: 14.1 us -> 22.9 us  [send(): return lax.ppermute(value, ('box', 'col'), pairs_of(boxes, route))]
  transfers between devices with their start and end apart: 17 -> 19, of which waited for: 5 -> 4; matrix products, arithmetic and copies ran while one was open for 0% -> 0% of each run, Pallas kernels for 39% -> 41%
where the time goes in v1:
time: 93.3 us; the launch traced here: 91.5 us
  Pallas kernels  44.2 us (47%)
  waiting for transfers between devices  22.9 us (25%)
  starting transfers between devices  20.6 us (22%)
  local copies, waits for them, and re-layouts  3.08 us (3%)
    ppermute x19, waiting for transfers between devices, send(): return lax.ppermute(value, ('box', 'col'), pairs_of(boxes, route))  22.9 us
    ppermute x19, starting transfers between devices, send(): return lax.ppermute(value, ('box', 'col'), pairs_of(boxes, route))  20.6 us
    pallas_call x1, Pallas kernels, body(): call(third_inverse_kernel, [square] * 3, [SMEM] + [VMEM] * 5, 10 << 30)  11.3 us
    pallas_call x1, Pallas kernels, body(): call(second_inverse_kernel, [square], [SMEM] + [VMEM] * 3, 10 << 30)  10.1 us
    pallas_call x1, Pallas kernels, body(): call(first_inverse_kernel, [square], [VMEM] * 2, 10 << 30)(s_own, s_peer)  9.55 us
    pallas_call x1, Pallas kernels, body(): call(final_kernel, [(4 * Q, Q)], [SMEM] * 2 + [VMEM] * 9 + [ANY] * 7, 4 <...  6.37 us
    pallas_call x1, Pallas kernels, body(): call(permute_kernel, [(Q, 2 * Q)] * 2, [SMEM, VMEM, VMEM], 1 << 30)  2.19 us
    unnamed x8, local copies, waits for them, and re-layouts  1.93 us
  transfers between devices with their start and end apart: 19, of which 4 were waited for; matrix products, arithmetic and copies ran while one was open for 0% of the time, Pallas kernels for 41%

profile of v1, /device:TPU:2, one launch (start us, length us, event | category | flops | bytes accessed | tf_op | source)
XLA Modules:
  0.0 91.5 jit_solution(15576805336620492074)
XLA Ops:
  0.0 1.1 %dynamic-slice_bitcast_fusion = (f32[256,256]{1,0:T(8,128)S(1)}, f32[256,256]{1,0:T(8,128)S(1)}) fusion(f32[1,1024,256]{2,1,0:T(8,128)} %param.3, s32[]{:T(128)S(6)} %select_n.33, s32[]{:T(128)S(6)} %select_n.32), kind=kLoop, calls=%fused_computation.1 | loop fusion | bytes 1048584 | tf_op jit(solution)/shard_map/dynamic_slice | solution.py:412
  1.1 0.0 copy-start.2
  1.1 0.7 collective-permute-start.5
  1.8 1.3 %collective-permute-start.6 = (f32[256,256]{1,0:T(8,128)S(1)}, f32[256,256]{1,0:T(8,128)S(1)}, u32[]{:S(2)}, u32[]{:S(2)}) collective-permute-start(f32[256,256]{1,0:T(8,128)S(1)} %get-tuple-element.27.raw), channel_id=1, source_target_pairs={{1,3},{2,0},{6,4},{7,5},{8,10},{9,11},{12,14},{15,13},{17,19},{18,... | collective-permute-start | bytes 786440 | tf_op jit(solution)/shard_map/ppermute | solution.py:378
  3.1 0.1 stack.35.role
  3.2 1.2 %copy-done = f32[1,1024,256]{2,1,0:T(8,128)S(1)} copy-done((f32[1,1024,256]{2,1,0:T(8,128)S(1)}, f32[1,1024,256]{2,1,0:T(8,128)}, u32[]{:S(2)}) %copy-start) | copy-done | bytes 1048600
  4.4 0.7 copy-done.1
  5.1 2.2 %shard_map.43 = (f32[256,512]{1,0:T(8,128)S(1)}, f32[256,512]{1,0:T(8,128)S(1)}) custom-call(s32[8]{0:T(128)S(1)} %stack.35.role, f32[1024,256]{1,0:T(8,128)S(1)} %bitcast.15, s32[4,256]{1,0:T(4,128)S(1)} %bitcast.16), custom_call_target="tpu_custom_call" | custom-call | flops 1073741824 | bytes 1048576 | tf_op jit(solution)/shard_map/pallas_call | solution.py:405
  7.3 6.4 %collective-permute-start.14 = (f32[256,512]{1,0:T(8,128)S(1)}, f32[256,512]{1,0:T(8,128)}, u32[]{:S(2)}, u32[]{:S(2)}) collective-permute-start(f32[256,512]{1,0:T(8,128)S(1)} %get-tuple-element.26), channel_id=1, source_target_pairs={{0,8},{1,13},{2,10},{3,15},{4,12},{5,9},{6,14},{7,11},{8,0},{9,5},... | collective-permute-start | bytes 1572872 | tf_op jit(solution)/shard_map/ppermute | solution.py:378
  13.7 1.3 %collective-permute-start.7 = (f32[256,256]{1,0:T(8,128)S(1)}, f32[256,256]{1,0:T(8,128)S(1)}, u32[]{:S(2)}, u32[]{:S(2)}) collective-permute-start(f32[256,256]{1,0:T(8,128)S(1)} %get-tuple-element.27.raw), channel_id=1, source_target_pairs={{1,0},{2,1},{6,5},{7,6},{8,11},{9,8},{12,15},{15,14},{17,16},{18,1... | collective-permute-start | bytes 786440 | tf_op jit(solution)/shard_map/ppermute | solution.py:378
  15.0 0.7 collective-permute-start
  15.7 0.7 collective-permute-start.1
  16.4 2.7 %collective-permute-done.6.g2 = f32[256,256]{1,0:T(8,128)S(1)} collective-permute-done((f32[256,256]{1,0:T(8,128)S(1)}, f32[256,256]{1,0:T(8,128)S(1)}, u32[]{:S(2)}, u32[]{:S(2)}) %collective-permute-start.6) | collective-permute-done | bytes 262176 | tf_op jit(solution)/shard_map/ppermute | solution.py:378
  19.1 1.3 %collective-permute-start.2 = (f32[256,256]{1,0:T(8,128)S(1)}, f32[256,256]{1,0:T(8,128)S(1)}, u32[]{:S(2)}, u32[]{:S(2)}) collective-permute-start(f32[256,256]{1,0:T(8,128)S(1)} %get-tuple-element.28.raw), channel_id=1, source_target_pairs={{1,0},{7,6},{9,8},{15,14},{17,16},{23,22},{25,24},{31,30},{33,32},... | collective-permute-start | bytes 786440 | tf_op jit(solution)/shard_map/ppermute | solution.py:378
  20.4 1.6 %collective-permute-done.7.g3 = f32[256,256]{1,0:T(8,128)S(1)} collective-permute-done((f32[256,256]{1,0:T(8,128)S(1)}, f32[256,256]{1,0:T(8,128)S(1)}, u32[]{:S(2)}, u32[]{:S(2)}) %collective-permute-start.7) | collective-permute-done | bytes 262176 | tf_op jit(solution)/shard_map/ppermute | solution.py:378
  22.0 1.6 %shard_map.39.own = f32[256,512]{1,0:T(8,128)S(1)} custom-call(s32[8]{0:T(128)S(1)} %stack.35.role, f32[256,256]{1,0:T(8,128)S(1)} %get-tuple-element.27.raw, f32[256,256]{1,0:T(8,128)S(1)} %collective-permute-done.5.g1, f32[256,256]{1,0:T(8,128)S(1)} %collective-permute-done.6.g2, f32[256,256]{1,0:T(8,128)S(1)} %collective-permute-done.7.g3, ...), custom_call_target="tpu_custom_call" | custom-call | flops 268435456 | bytes 1048576 | tf_op jit(solution)/shard_map/pallas_call | solution.py:425
  23.6 0.1 collective-permute-start.8
  23.7 0.0 collective-permute-done.g1
  23.7 3.9 %collective-permute-done.2.g3 = f32[256,256]{1,0:T(8,128)S(1)} collective-permute-done((f32[256,256]{1,0:T(8,128)S(1)}, f32[256,256]{1,0:T(8,128)S(1)}, u32[]{:S(2)}, u32[]{:S(2)}) %collective-permute-start.2) | collective-permute-done | bytes 262176 | tf_op jit(solution)/shard_map/ppermute | solution.py:378
  27.6 1.2 %shard_map.37.s_own = f32[256,256]{1,0:T(8,128)S(1)} custom-call(s32[8]{0:T(128)S(1)} %stack.35.role, f32[256,256]{1,0:T(8,128)S(1)} %get-tuple-element.28.raw, f32[256,256]{1,0:T(8,128)S(1)} %collective-permute-done.g1, f32[256,256]{1,0:T(8,128)S(1)} %collective-permute-done.1.g2, f32[256,256]{1,0:T(8,128)S(1)} %collective-permute-done.2.g3, ...), custom_call_target="tpu_custom_call" | custom-call | flops 268435456 | bytes 1048576 | tf_op jit(solution)/shard_map/pallas_call | solution.py:406
  28.8 0.1 collective-permute-start.3
  28.9 0.0 collective-permute-done.14
  28.9 0.1 broadcast_select_fusion.e_own
  29.0 1.9 %collective-permute-start.15 = (f32[256,512]{1,0:T(8,128)S(1)}, f32[256,512]{1,0:T(8,128)S(1)}, u32[]{:S(2)}, u32[]{:S(2)}) collective-permute-start(f32[256,512]{1,0:T(8,128)S(1)} %broadcast_select_fusion.e_own), channel_id=1, source_target_pairs={{0,1},{1,0},{2,3},{3,2},{4,5},{5,4},{6,7},{7,6},{8,9},{9,8},{10,11... | collective-permute-start | bytes 1572872 | tf_op jit(solution)/shard_map/ppermute | solution.py:378
  30.9 0.2 collective-permute-start.16
  31.0 0.0 collective-permute-start.17
  31.0 0.0 collective-permute-done.3.s_peer
  31.0 9.6 %shard_map.38.inv.inv_own = f32[256,256]{1,0:T(8,128)S(1)} custom-call(f32[256,256]{1,0:T(8,128)S(1)} %shard_map.37.s_own, f32[256,256]{1,0:T(8,128)S(1)} %collective-permute-done.3.s_peer), custom_call_target="tpu_custom_call" | custom-call | flops 10737418240 | bytes 1048576 | tf_op jit(solution)/shard_map/pallas_call | solution.py:423
  40.6 0.0 collective-permute-done.8.peer
  40.6 1.9 %shard_map.40 = (f32[512,256]{1,0:T(8,128)S(1)}, f32[256,256]{1,0:T(8,128)S(1)}, f32[128,256]{1,0:T(8,128)S(1)}, f32[512,256]{1,0:T(8,128)S(1)}, f32[256,256]{1,0:T(8,128)S(1)}, /*index=5*/f32[256,256]{1,0:T(8,128)S(1)}) custom-call(s32[8]{0:T(128)S(1)} %stack.35.role, f32[256,256]{1,0:T(8,128)S(1)} %shard_map.38.inv.inv_own, f32[256,512]{1,0:T(8,128)S(1)} %shard_map.39.own, ...), custom_call_target="tpu_custom_call" | custom-call | flops 2147483648 | bytes 1048576 | tf_op jit(solution)/shard_map/pallas_call | solution.py:435
  42.5 3.3 %collective-permute-start.9 = (f32[512,256]{1,0:T(8,128)S(1)}, f32[512,256]{1,0:T(8,128)S(1)}, u32[]{:S(2)}, u32[]{:S(2)}) collective-permute-start(f32[512,256]{1,0:T(8,128)S(1)} %get-tuple-element.17), channel_id=1, source_target_pairs={{0,8},{1,9},{2,10},{3,11},{4,12},{5,13},{6,14},{7,15},{8,0},{9,1},... | collective-permute-start | bytes 1572872 | tf_op jit(solution)/shard_map/ppermute | solution.py:378
  45.8 0.1 collective-permute-start.11
  45.9 14.7 %collective-permute-done.11.far = f32[128,256]{1,0:T(8,128)S(1)} collective-permute-done((f32[128,256]{1,0:T(8,128)S(1)}, f32[128,256]{1,0:T(8,128)S(1)}, u32[]{:S(2)}, u32[]{:S(2)}) %collective-permute-start.11) | collective-permute-done | bytes 131104 | tf_op jit(solution)/shard_map/ppermute | solution.py:378
  60.6 0.0 collective-permute-start.12
  60.6 0.0 collective-permute-done.15.r0
  60.6 0.0 collective-permute-done.16.r1
  60.6 0.2 pad_maximum_fusion
  60.8 0.6 collective-permute-start.18
  61.4 1.7 %collective-permute-start.13 = (f32[256,512]{1,0:T(8,128)S(1)}, f32[256,512]{1,0:T(8,128)S(1)}, u32[]{:S(2)}, u32[]{:S(2)}) collective-permute-start(f32[256,512]{1,0:T(8,128)S(1)} %get-tuple-element.25.d_own), channel_id=1, source_target_pairs={{0,8},{1,5},{2,10},{3,7},{4,12},{5,1},{6,14},{7,3},{8,0},{9,13},{1... | collective-permute-start | bytes 1572872 | tf_op jit(solution)/shard_map/ppermute | solution.py:378
  63.1 0.3 collective-permute-start.4
  63.4 0.0 collective-permute-done.9.far.zt_far
  63.4 0.0 collective-permute-start.10
  63.4 0.0 collective-permute-done.12.far_peer
  63.4 10.1 %shard_map.41.inv0 = f32[256,256]{1,0:T(8,128)S(1)} custom-call(s32[8]{0:T(128)S(1)} %stack.35.role, f32[256,256]{1,0:T(8,128)S(1)} %get-tuple-element.18.c_own, f32[128,256]{1,0:T(8,128)S(1)} %collective-permute-done.11.far, f32[128,256]{1,0:T(8,128)S(1)} %collective-permute-done.12.far_peer), custom_call_target="tpu_custom_call" | custom-call | flops 10737418240 | bytes 1048576 | tf_op jit(solution)/shard_map/pallas_call | solution.py:447
  73.5 0.0 collective-permute-done.10.far_peer.zt_far_peer
  73.5 0.0 copy-start.3
  73.5 11.3 %shard_map.42 = (f32[256,256]{1,0:T(8,128)S(1)}, f32[256,256]{1,0:T(8,128)S(1)}, f32[256,256]{1,0:T(8,128)S(1)}) custom-call(s32[8]{0:T(128)S(1)} %stack.35.role, f32[256,256]{1,0:T(8,128)S(1)} %shard_map.41.inv0, f32[256,256]{1,0:T(8,128)S(1)} %get-tuple-element.20.c01, f32[256,256]{1,0:T(8,128)S(1)} %get-tuple-element.21.c11, ...), custom_call_target="tpu_custom_call" | custom-call | flops 10737418240 | bytes 1048576 | tf_op jit(solution)/shard_map/pallas_call | solution.py:448
  84.9 6.4 %shard_map.44 = f32[1024,256]{1,0:T(8,128)} custom-call(s32[8]{0:T(128)S(1)} %stack.35.role, s32[80]{0:T(128)S(1)} %copy-done.3, f32[256,256]{1,0:T(8,128)S(1)} %shard_map.38.inv.inv_own, f32[256,256]{1,0:T(8,128)S(1)} %collective-permute-done.4.inv_far, f32[512,256]{1,0:T(8,128)S(1)} %get-tuple-element.16.zt_own, ...), custom_call_target="tpu_custom_call" | custom-call | flops 4294967296 | bytes 1048576 | tf_op jit(solution)/shard_map/pallas_call | solution.py:451
  (10 shorter events, 0.0 us)
Async XLA Ops:
  1.1 20.9 %copy-start.2 = (s32[1,4,256]{2,1,0:T(4,128)S(1)}, s32[1,4,256]{2,1,0:T(4,128)}, u32[]{:S(2)}) copy-start(s32[1,4,256]{2,1,0:T(4,128)} %param.4) | copy-start | bytes 12292
  1.1 14.6 %collective-permute-start.5 = (f32[256,256]{1,0:T(8,128)S(1)}, f32[256,256]{1,0:T(8,128)S(1)}, u32[]{:S(2)}, u32[]{:S(2)}) collective-permute-start(f32[256,256]{1,0:T(8,128)S(1)} %get-tuple-element.27.raw), channel_id=1, source_target_pairs={{1,2},{2,3},{6,7},{7,4},{8,9},{9,10},{12,13},{15,12},{17,18},{18,1... | collective-permute-start | bytes 786440 | tf_op jit(solution)/shard_map/ppermute | solution.py:378
  1.8 17.4 %collective-permute-start.6 = (f32[256,256]{1,0:T(8,128)S(1)}, f32[256,256]{1,0:T(8,128)S(1)}, u32[]{:S(2)}, u32[]{:S(2)}) collective-permute-start(f32[256,256]{1,0:T(8,128)S(1)} %get-tuple-element.27.raw), channel_id=1, source_target_pairs={{1,3},{2,0},{6,4},{7,5},{8,10},{9,11},{12,14},{15,13},{17,19},{18,... | collective-permute-start | bytes 786440 | tf_op jit(solution)/shard_map/ppermute | solution.py:378
  3.2 1.2 %copy-start = (f32[1,1024,256]{2,1,0:T(8,128)S(1)}, f32[1,1024,256]{2,1,0:T(8,128)}, u32[]{:S(2)}) copy-start(f32[1,1024,256]{2,1,0:T(8,128)} %param.3) | copy-start | bytes 3145732
  4.4 0.7 copy-start.1
  7.3 21.6 %collective-permute-start.14 = (f32[256,512]{1,0:T(8,128)S(1)}, f32[256,512]{1,0:T(8,128)}, u32[]{:S(2)}, u32[]{:S(2)}) collective-permute-start(f32[256,512]{1,0:T(8,128)S(1)} %get-tuple-element.26), channel_id=1, source_target_pairs={{0,8},{1,13},{2,10},{3,15},{4,12},{5,9},{6,14},{7,11},{8,0},{9,5},... | collective-permute-start | bytes 1572872 | tf_op jit(solution)/shard_map/ppermute | solution.py:378
  13.7 8.3 %collective-permute-start.7 = (f32[256,256]{1,0:T(8,128)S(1)}, f32[256,256]{1,0:T(8,128)S(1)}, u32[]{:S(2)}, u32[]{:S(2)}) collective-permute-start(f32[256,256]{1,0:T(8,128)S(1)} %get-tuple-element.27.raw), channel_id=1, source_target_pairs={{1,0},{2,1},{6,5},{7,6},{8,11},{9,8},{12,15},{15,14},{17,16},{18,1... | collective-permute-start | bytes 786440 | tf_op jit(solution)/shard_map/ppermute | solution.py:378
  15.0 8.7 %collective-permute-start = (f32[256,256]{1,0:T(8,128)S(1)}, f32[256,256]{1,0:T(8,128)S(1)}, u32[]{:S(2)}, u32[]{:S(2)}) collective-permute-start(f32[256,256]{1,0:T(8,128)S(1)} %get-tuple-element.28.raw), channel_id=1, source_target_pairs={{1,2},{7,4},{9,10},{15,12},{17,18},{23,20},{25,26},{31,28},{33,34}... | collective-permute-start | bytes 786440 | tf_op jit(solution)/shard_map/ppermute | solution.py:378
  15.7 8.0 %collective-permute-start.1 = (f32[256,256]{1,0:T(8,128)S(1)}, f32[256,256]{1,0:T(8,128)S(1)}, u32[]{:S(2)}, u32[]{:S(2)}) collective-permute-start(f32[256,256]{1,0:T(8,128)S(1)} %get-tuple-element.28.raw), channel_id=1, source_target_pairs={{1,3},{7,5},{9,11},{15,13},{17,19},{23,21},{25,27},{31,29},{33,35}... | collective-permute-start | bytes 786440 | tf_op jit(solution)/shard_map/ppermute | solution.py:378
  19.1 8.5 %collective-permute-start.2 = (f32[256,256]{1,0:T(8,128)S(1)}, f32[256,256]{1,0:T(8,128)S(1)}, u32[]{:S(2)}, u32[]{:S(2)}) collective-permute-start(f32[256,256]{1,0:T(8,128)S(1)} %get-tuple-element.28.raw), channel_id=1, source_target_pairs={{1,0},{7,6},{9,8},{15,14},{17,16},{23,22},{25,24},{31,30},{33,32},... | collective-permute-start | bytes 786440 | tf_op jit(solution)/shard_map/ppermute | solution.py:378
  23.6 17.0 %collective-permute-start.8 = (f32[256,512]{1,0:T(8,128)S(1)}, f32[256,512]{1,0:T(8,128)S(1)}, u32[]{:S(2)}, u32[]{:S(2)}) collective-permute-start(f32[256,512]{1,0:T(8,128)S(1)} %shard_map.39.own), channel_id=1, source_target_pairs={{0,4},{1,5},{2,6},{3,7},{4,0},{5,1},{6,2},{7,3},{8,12},{9,13},{10,... | collective-permute-start | bytes 1572872 | tf_op jit(solution)/shard_map/ppermute | solution.py:378
  28.8 2.2 %collective-permute-start.3 = (f32[256,256]{1,0:T(8,128)S(1)}, f32[256,256]{1,0:T(8,128)S(1)}, u32[]{:S(2)}, u32[]{:S(2)}) collective-permute-start(f32[256,256]{1,0:T(8,128)S(1)} %shard_map.37.s_own), channel_id=1, source_target_pairs={{0,4},{1,5},{2,6},{3,7},{4,0},{5,1},{6,2},{7,3},{8,12},{9,13},{10,... | collective-permute-start | bytes 786440 | tf_op jit(solution)/shard_map/ppermute | solution.py:378
  29.0 31.6 %collective-permute-start.15 = (f32[256,512]{1,0:T(8,128)S(1)}, f32[256,512]{1,0:T(8,128)S(1)}, u32[]{:S(2)}, u32[]{:S(2)}) collective-permute-start(f32[256,512]{1,0:T(8,128)S(1)} %broadcast_select_fusion.e_own), channel_id=1, source_target_pairs={{0,1},{1,0},{2,3},{3,2},{4,5},{5,4},{6,7},{7,6},{8,9},{9,8},{10,11... | collective-permute-start | bytes 1572872 | tf_op jit(solution)/shard_map/ppermute | solution.py:378
  30.9 29.7 %collective-permute-start.16 = (f32[256,512]{1,0:T(8,128)S(1)}, f32[256,512]{1,0:T(8,128)S(1)}, u32[]{:S(2)}, u32[]{:S(2)}) collective-permute-start(f32[256,512]{1,0:T(8,128)S(1)} %broadcast_select_fusion.e_own), channel_id=1, source_target_pairs={{0,3},{1,2},{2,1},{3,0},{4,7},{5,6},{6,5},{7,4},{8,11},{9,10},{10,... | collective-permute-start | bytes 1572872 | tf_op jit(solution)/shard_map/ppermute | solution.py:378
  31.0 29.6 %collective-permute-start.17 = (f32[256,512]{1,0:T(8,128)S(1)}, f32[256,512]{1,0:T(8,128)S(1)}, u32[]{:S(2)}, u32[]{:S(2)}) collective-permute-start(f32[256,512]{1,0:T(8,128)S(1)} %broadcast_select_fusion.e_own), channel_id=1, source_target_pairs={{0,4},{1,3},{2,6},{3,1},{4,0},{5,7},{6,2},{7,5},{8,10},{9,11},{10,... | collective-permute-start | bytes 1572872 | tf_op jit(solution)/shard_map/ppermute | solution.py:378
  42.5 20.9 %collective-permute-start.9 = (f32[512,256]{1,0:T(8,128)S(1)}, f32[512,256]{1,0:T(8,128)S(1)}, u32[]{:S(2)}, u32[]{:S(2)}) collective-permute-start(f32[512,256]{1,0:T(8,128)S(1)} %get-tuple-element.17), channel_id=1, source_target_pairs={{0,8},{1,9},{2,10},{3,11},{4,12},{5,13},{6,14},{7,15},{8,0},{9,1},... | collective-permute-start | bytes 1572872 | tf_op jit(solution)/shard_map/ppermute | solution.py:378
  45.8 14.8 %collective-permute-start.11 = (f32[128,256]{1,0:T(8,128)S(1)}, f32[128,256]{1,0:T(8,128)S(1)}, u32[]{:S(2)}, u32[]{:S(2)}) collective-permute-start(f32[128,256]{1,0:T(8,128)S(1)} %get-tuple-element.19), channel_id=1, source_target_pairs={{0,8},{1,9},{2,10},{3,11},{4,12},{5,13},{6,14},{7,15},{8,0},{9,1},... | collective-permute-start | bytes 393224 | tf_op jit(solution)/shard_map/ppermute | solution.py:378
  60.6 2.8 %collective-permute-start.12 = (f32[128,256]{1,0:T(8,128)S(1)}, f32[128,256]{1,0:T(8,128)S(1)}, u32[]{:S(2)}, u32[]{:S(2)}) collective-permute-start(f32[128,256]{1,0:T(8,128)S(1)} %collective-permute-done.11.far), channel_id=1, source_target_pairs={{0,4},{1,5},{2,6},{3,7},{4,0},{5,1},{6,2},{7,3},{8,12},{9,13},{10,... | collective-permute-start | bytes 393224 | tf_op jit(solution)/shard_map/ppermute | solution.py:378
  60.8 24.1 %collective-permute-start.18 = (f32[1024,512]{1,0:T(8,128)S(1)}, f32[1024,512]{1,0:T(8,128)S(1)}, u32[]{:S(2)}, u32[]{:S(2)}) collective-permute-start(f32[1024,512]{1,0:T(8,128)S(1)} %pad_maximum_fusion), channel_id=1, source_target_pairs={{0,4},{1,5},{2,6},{3,7},{4,0},{5,1},{6,2},{7,3},{8,12},{9,13},{10,... | collective-permute-start | bytes 6291464 | tf_op jit(solution)/shard_map/ppermute | solution.py:378
  61.4 23.5 %collective-permute-start.13 = (f32[256,512]{1,0:T(8,128)S(1)}, f32[256,512]{1,0:T(8,128)S(1)}, u32[]{:S(2)}, u32[]{:S(2)}) collective-permute-start(f32[256,512]{1,0:T(8,128)S(1)} %get-tuple-element.25.d_own), channel_id=1, source_target_pairs={{0,8},{1,5},{2,10},{3,7},{4,12},{5,1},{6,14},{7,3},{8,0},{9,13},{1... | collective-permute-start | bytes 1572872 | tf_op jit(solution)/shard_map/ppermute | solution.py:378
  63.1 21.8 %collective-permute-start.4 = (f32[256,256]{1,0:T(8,128)S(1)}, f32[256,256]{1,0:T(8,128)S(1)}, u32[]{:S(2)}, u32[]{:S(2)}) collective-permute-start(f32[256,256]{1,0:T(8,128)S(1)} %shard_map.38.inv.inv_own), channel_id=1, source_target_pairs={{0,8},{1,5},{2,10},{3,7},{4,12},{5,1},{6,14},{7,3},{8,0},{9,13},{1... | collective-permute-start | bytes 786440 | tf_op jit(solution)/shard_map/ppermute | solution.py:378
  63.4 10.1 %collective-permute-start.10 = (f32[512,256]{1,0:T(8,128)S(1)}, f32[512,256]{1,0:T(8,128)S(1)}, u32[]{:S(2)}, u32[]{:S(2)}) collective-permute-start(f32[512,256]{1,0:T(8,128)S(1)} %collective-permute-done.9.far.zt_far), channel_id=1, source_target_pairs={{0,4},{1,5},{2,6},{3,7},{4,0},{5,1},{6,2},{7,3},{8,12},{9,13},{10,... | collective-permute-start | bytes 1572872 | tf_op jit(solution)/shard_map/ppermute | solution.py:378
  73.5 11.4 %copy-start.3 = (s32[80]{0:T(128)S(1)}, s32[80]{0:T(128)}, u32[]{:S(2)}) copy-start(s32[80]{0:T(128)} %constant.49.clone.table) | copy-start | bytes 964
